TPU v7x, 32 devices: a whole 2x2x4 slice. The times are simulated.
32 devices in a mesh: gx: 4 (over y, core), gy: 8 (over z, x).
Axes of the slice: x: 2, y: 2, z: 4, core: 2. Of those that a mesh axis runs over, the one named last changes fastest.
Arguments:
- source: float32 [256, 128, 128], P('gx', 'gy'), may hold values from -6 to 6
- diagonal: float32 [256, 128, 128], P('gx', 'gy'), may hold values from 6.05 to 7
- face_x: float32 [256, 128, 128], P('gx', 'gy'), may hold values from 0.1 to 1
- face_y: float32 [256, 128, 128], P('gx', 'gy'), may hold values from 0.1 to 1
- face_z: float32 [256, 128, 128], P('gx', 'gy'), may hold values from 0.1 to 1
- iterates: float32 [8, 256, 128, 128], P(None, 'gx', 'gy'), may hold values from -0.3 to 0.3
- labels: int32 [256, 128], P('gx', 'gy'), may hold values from 0 to 7
Outputs:
- new_iterates: float32 [8, 256, 128, 128], P(None, 'gx', 'gy')
- new_residual: float32 [256, 128, 128], P('gx', 'gy')
All inputs are finite; a program needn't handle non-finite values.
Results may differ from a plain program's by a relative error of at most 0.0003.
Values sent between devices are 32-bit elements; how exact they have to be, the bound alone decides.
No kernel may reach another device: no remote copies, remote signals or barrier semaphores. Data moves between devices by JAX's collectives and lax.ppermute only.
A program may use at most 128 MiB of HBM per device.

v0:
```python
import jax
import jax.numpy as jnp
from jax import lax
from jax.sharding import PartitionSpec as P

ENLARGE = 8
basis_shift = 6.5


def padded_2(block, sides, width):
    for axis, dim in sides:
        count = lax.axis_size(axis)
        forward = [(i, i + 1) for i in range(count - 1)]
        backward = [(target, source) for source, target in forward]
        low = lax.ppermute(
            lax.slice_in_dim(block, block.shape[dim] - width, None, axis=dim), axis, forward
        )
        high = lax.ppermute(lax.slice_in_dim(block, 0, width, axis=dim), axis, backward)
        block = jnp.concatenate([low, block, high], axis=dim)
    return block


def stencil(values, face_x, face_y, face_z, diagonal):
    centre = values[..., 1:-1, 1:-1, :]
    result = diagonal * centre
    result = (
        result
        - face_x[1:-1, 1:-1, :] * values[..., 2:, 1:-1, :]
        - face_x[:-2, 1:-1, :] * values[..., :-2, 1:-1, :]
    )
    result = (
        result
        - face_y[1:-1, 1:-1, :] * values[..., 1:-1, 2:, :]
        - face_y[1:-1, :-2, :] * values[..., 1:-1, :-2, :]
    )
    widths = [(0, 0)] * (centre.ndim - 1) + [(1, 1)]
    padded = jnp.pad(centre, widths)
    lower_face = jnp.pad(face_z[..., :-1], ((0, 0), (0, 0), (1, 0)))
    return result - face_z * padded[..., 2:] - lower_face * padded[..., :-2]


def finish(gram, project):
    highest = lax.Precision.HIGHEST
    lower = jnp.linalg.cholesky(gram)
    ident = jnp.eye(gram.shape[0], dtype=gram.dtype)
    inverse = lax.linalg.triangular_solve(lower, ident, left_side=True, lower=True)
    reduced = jnp.dot(jnp.dot(inverse, project, precision=highest), inverse.T, precision=highest)
    reduced = 0.5 * (reduced + reduced.T)
    target = jnp.dot(inverse, gram[:, :ENLARGE], precision=highest)
    factor = jnp.linalg.cholesky(reduced)
    middle = lax.linalg.triangular_solve(factor, target, left_side=True, lower=True)
    solved = lax.linalg.triangular_solve(
        factor, middle, left_side=True, lower=True, transpose_a=True
    )
    return jnp.dot(inverse.T, solved, precision=highest)


def shards(source, diagonal, face_x, face_y, face_z, iterates, labels):
    highest = lax.Precision.HIGHEST
    summed = jnp.sum(iterates, axis=0)
    columns = jnp.arange(ENLARGE, dtype=jnp.int32)
    near = (
        padded_2(summed, (("gx", 0), ("gy", 1)), 1),
        padded_2(face_x, (("gx", 0), ("gy", 1)), 1),
        padded_2(face_y, (("gx", 0), ("gy", 1)), 1),
    )
    near_sum, near_fx, near_fy = near
    residual = source - stencil(near_sum, near_fx, near_fy, face_z, diagonal)
    onehot = (labels[None] == columns[:, None, None]).astype(jnp.float32)
    blocks = residual[None] * onehot[..., None]
    blocks_wide = padded_2(blocks, (("gx", 1), ("gy", 2)), 1)
    applied = stencil(blocks_wide, near_fx, near_fy, face_z, diagonal)
    powered = applied - basis_shift * blocks
    powered_wide = padded_2(powered, (("gx", 1), ("gy", 2)), 1)
    second = stencil(powered_wide, near_fx, near_fy, face_z, diagonal)
    basis = jnp.concatenate([blocks, powered], axis=0)
    image = jnp.concatenate([applied, second], axis=0)
    gram_local = jnp.einsum("aijk,bijk->ab", basis, basis, precision=highest)
    project_local = jnp.einsum("aijk,bijk->ab", basis, image, precision=highest)
    gram = lax.psum(gram_local, ("gx", "gy"))
    project = lax.psum(project_local, ("gx", "gy"))
    coeffs = finish(gram, project)
    new_iterates = iterates + jnp.einsum("ab,aijk->bijk", coeffs, basis, precision=highest)
    carried = jnp.sum(coeffs, axis=1)
    new_residual = residual - jnp.einsum("a,aijk->ijk", carried, image, precision=highest)
    return (new_iterates, new_residual)


def solution(mesh):
    placed = (
        P("gx", "gy", None),
        P("gx", "gy", None),
        P("gx", "gy", None),
        P("gx", "gy", None),
        P("gx", "gy", None),
        P(None, "gx", "gy", None),
        P("gx", "gy"),
    )
    return jax.shard_map(
        shards,
        mesh=mesh,
        in_specs=placed,
        out_specs=(P(None, "gx", "gy", None), P("gx", "gy", None)),
        check_vma=False,
    )
```

profile of v0, /device:TPU:0, one launch (start us, length us, event | category | flops | bytes accessed | tf_op | source)
XLA Modules:
  0.0 177.3 jit_solution(15040397435094770270)
XLA Ops:
  0.7 2.7 %reduce_sum.18 = f32[64,16,128]{2,1,0:T(8,128)S(1)} reduce(f32[8,64,16,128]{3,2,1,0:T(8,128)} %param.13, f32[]{:T(128)} %constant.43.clone.1), dimensions={0}, to_apply=%region_0.0 | reduce | flops 917504 | bytes 4718596 | tf_op jit(solution)/shard_map/reduce_sum | solution.py:60
  3.4 1.3 collective-permute-start
  4.7 3.0 %collective-permute-start.2 = (f32[1,16,128]{2,1,0:T(8,128)S(1)}, f32[1,16,128]{2,1,0:T(8,128)S(1)}, u32[]{:S(2)}, u32[]{:S(2)}) collective-permute-start(f32[1,16,128]{2,1,0:T(8,128)S(1)} %get-tuple-element.23), channel_id=1, source_target_pairs={{0,8},{8,16},{16,24},{1,9},{9,17},{17,25},{2,10},{10,18},{18,26},{... | collective-permute-start | bytes 24584 | tf_op jit(solution)/shard_map/ppermute | solution.py:15
  7.7 4.5 %collective-permute-start.4 = (f32[1,16,128]{2,1,0:T(8,128)S(1)}, f32[1,16,128]{2,1,0:T(8,128)S(1)}, u32[]{:S(2)}, u32[]{:S(2)}) collective-permute-start(f32[1,16,128]{2,1,0:T(8,128)S(1)} %get-tuple-element.22), channel_id=1, source_target_pairs={{0,8},{8,16},{16,24},{1,9},{9,17},{17,25},{2,10},{10,18},{18,26},{... | collective-permute-start | bytes 24584 | tf_op jit(solution)/shard_map/ppermute | solution.py:15
  12.2 1.3 collective-permute-start.5
  13.6 3.0 %collective-permute-start.1 = (f32[1,16,128]{2,1,0:T(8,128)S(1)}, f32[1,16,128]{2,1,0:T(8,128)S(1)}, u32[]{:S(2)}, u32[]{:S(2)}) collective-permute-start(f32[1,16,128]{2,1,0:T(8,128)S(1)} %slice.156), channel_id=1, source_target_pairs={{0,8},{8,16},{16,24},{1,9},{9,17},{17,25},{2,10},{10,18},{18,26},{... | collective-permute-start | bytes 24584 | tf_op jit(solution)/shard_map/ppermute | solution.py:15
  16.8 1.3 collective-permute-start.3
  18.1 4.5 %collective-permute-start.7 = (f32[66,1,128]{2,1,0:T(1,128)S(1)}, f32[66,1,128]{2,1,0:T(1,128)S(1)}, u32[]{:S(2)}, u32[]{:S(2)}) collective-permute-start(f32[66,1,128]{2,1,0:T(1,128)S(1)} %get-tuple-element.20), channel_id=1, source_target_pairs={{0,1},{1,2},{2,3},{3,4},{4,5},{5,6},{6,7},{8,9},{9,10},{10,11},{11... | collective-permute-start | bytes 101384 | tf_op jit(solution)/shard_map/ppermute | solution.py:15
  22.7 4.3 %collective-permute-start.6 = (f32[66,1,128]{2,1,0:T(1,128)S(1)}, f32[66,1,128]{2,1,0:T(1,128)S(1)}, u32[]{:S(2)}, u32[]{:S(2)}) collective-permute-start(f32[66,1,128]{2,1,0:T(1,128)S(1)} %slice.194), channel_id=1, source_target_pairs={{0,1},{1,2},{2,3},{3,4},{4,5},{5,6},{6,7},{8,9},{9,10},{10,11},{11... | collective-permute-start | bytes 101384 | tf_op jit(solution)/shard_map/ppermute | solution.py:15
  27.1 0.2 fusion.43
  27.3 1.3 collective-permute-done.6
  28.6 1.6 fusion.33
  30.2 1.3 broadcast_multiply_fusion
  31.5 1.3 collective-permute-start.8
  32.8 3.0 %collective-permute-start.9 = (f32[8,1,16,128]{3,0,2,1:T(8,128)S(1)}, f32[8,1,16,128]{3,0,2,1:T(8,128)S(1)}, u32[]{:S(2)}, u32[]{:S(2)}) collective-permute-start(f32[8,1,16,128]{3,0,2,1:T(8,128)S(1)} %get-tuple-element.17), channel_id=1, source_target_pairs={{0,8},{8,16},{16,24},{1,9},{9,17},{17,25},{2,10},{10,18},{18,26},{... | collective-permute-start | bytes 196616 | tf_op jit(solution)/shard_map/ppermute | solution.py:15
  35.9 0.9 collective-permute-done.9
  36.8 1.3 collective-permute-start.10
  38.1 5.0 %collective-permute-start.11 = (f32[8,66,1,128]{3,0,2,1:T(8,128)S(1)}, f32[8,66,1,128]{3,0,2,1:T(8,128)S(1)}, u32[]{:S(2)}, u32[]{:S(2)}) collective-permute-start(f32[8,66,1,128]{3,0,2,1:T(8,128)S(1)} %get-tuple-element.14), channel_id=1, source_target_pairs={{0,1},{1,2},{2,3},{3,4},{4,5},{5,6},{6,7},{8,9},{9,10},{10,11},{11... | collective-permute-start | bytes 811016 | tf_op jit(solution)/shard_map/ppermute | solution.py:15
  43.1 0.2 pad.18
  43.4 4.0 %collective-permute-done.10 = f32[8,66,1,128]{3,0,2,1:T(8,128)S(1)} collective-permute-done((f32[8,66,1,128]{3,0,2,1:T(8,128)S(1)}, f32[8,66,1,128]{3,0,2,1:T(8,128)S(1)}, u32[]{:S(2)}, u32[]{:S(2)}) %collective-permute-start.10) | collective-permute-done | bytes 270368 | tf_op jit(solution)/shard_map/ppermute | solution.py:18
  47.4 7.2 %collective-permute-done.11 = f32[8,66,1,128]{3,0,2,1:T(8,128)S(1)} collective-permute-done((f32[8,66,1,128]{3,0,2,1:T(8,128)S(1)}, f32[8,66,1,128]{3,0,2,1:T(8,128)S(1)}, u32[]{:S(2)}, u32[]{:S(2)}) %collective-permute-start.11) | collective-permute-done | bytes 270368 | tf_op jit(solution)/shard_map/ppermute | solution.py:15
  54.6 7.5 %multiply_subtract_fusion = (f32[8,64,16,128]{3,0,2,1:T(8,128)S(1)}, f32[8,64,16,128]{3,0,2,1:T(8,128)S(1)}) fusion(f32[8,64,16]{0,2,1:T(8,128)S(1)} %fusion.43, f32[64,16,128]{2,1,0:T(8,128)S(1)} %get-tuple-element.9, f32[64,16,128]{2,1,0:T(8,128)S(1)} %pad.18, f32[8,64,16,128]{3,0,2,1:T(8,128)S(1)} %broadcast_multiply_fusion, ...), kind=kLoop, calls=%fused_computation.51 | loop fusion | flops 25165824 | bytes 17481728 | tf_op jit(solution)/shard_map/sub | solution.py:73
  62.1 1.3 collective-permute-start.12
  63.4 3.0 %collective-permute-start.13 = (f32[8,1,16,128]{3,0,2,1:T(8,128)S(1)}, f32[8,1,16,128]{3,0,2,1:T(8,128)S(1)}, u32[]{:S(2)}, u32[]{:S(2)}) collective-permute-start(f32[8,1,16,128]{3,0,2,1:T(8,128)S(1)} %get-tuple-element.15), channel_id=1, source_target_pairs={{0,8},{8,16},{16,24},{1,9},{9,17},{17,25},{2,10},{10,18},{18,26},{... | collective-permute-start | bytes 196616 | tf_op jit(solution)/shard_map/ppermute | solution.py:15
  66.5 0.9 collective-permute-done.13
  67.4 1.3 collective-permute-start.14
  68.7 5.0 %collective-permute-start.15 = (f32[8,66,1,128]{3,0,2,1:T(8,128)S(1)}, f32[8,66,1,128]{3,0,2,1:T(8,128)S(1)}, u32[]{:S(2)}, u32[]{:S(2)}) collective-permute-start(f32[8,66,1,128]{3,0,2,1:T(8,128)S(1)} %get-tuple-element.12), channel_id=1, source_target_pairs={{0,1},{1,2},{2,3},{3,4},{4,5},{5,6},{6,7},{8,9},{9,10},{10,11},{11... | collective-permute-start | bytes 811016 | tf_op jit(solution)/shard_map/ppermute | solution.py:15
  73.7 11.2 %fusion.28 = f32[16,16]{0,1:T(8,128)S(1)} fusion(f32[8,64,16,128]{3,0,2,1:T(8,128)S(1)} %get-tuple-element.7, f32[8,64,16,128]{3,0,2,1:T(8,128)S(1)} %broadcast_multiply_fusion), kind=kOutput, calls=%fused_computation.55 | convolution fusion | flops 404750336 | bytes 8389632 | tf_op jit(solution)/shard_map/aijk,bijk->ab/dot_general | solution.py:78
  84.9 0.4 collective-permute-done.15
  85.3 6.8 %fusion.10 = f32[8,64,16,128]{3,0,2,1:T(8,128)S(1)} fusion(f32[8,64,16,128]{3,0,2,1:T(8,128)S(1)} %get-tuple-element.7, f32[8,66,1,128]{3,0,2,1:T(8,128)S(1)} %collective-permute-done.15, f32[8,1,16,128]{3,0,2,1:T(8,128)S(1)} %collective-permute-done.12, f32[8,1,16,128]{3,0,2,1:T(8,128)S(1)} %collective-permute-done.13, ...), kind=kLoop, calls=%fused_computation.16 | loop fusion | flops 22020096 | bytes 12730368 | tf_op jit(solution)/shard_map/sub | solution.py:39
  92.1 1.9 %copy-done.5 = f32[8,64,16,128]{3,0,2,1:T(8,128)} copy-done((f32[8,64,16,128]{3,0,2,1:T(8,128)}, f32[8,64,16,128]{3,0,2,1:T(8,128)S(1)}, u32[]{:S(2)}) %copy-start.5) | copy-done | bytes 4194328
  94.1 10.4 %fusion.29 = f32[16,16]{1,0:T(8,128)S(1)} fusion(f32[8,64,16,128]{3,0,2,1:T(8,128)S(1)} %fusion.10, f32[8,64,16,128]{3,0,2,1:T(8,128)S(1)} %get-tuple-element.8, f32[8,64,16,128]{3,0,2,1:T(8,128)S(1)} %get-tuple-element.7, f32[8,64,16,128]{3,0,2,1:T(8,128)S(1)} %broadcast_multiply_fusion), kind=kOutput, calls=%fused_computation.56 | convolution fusion | flops 406847488 | bytes 16778240 | tf_op jit(solution)/shard_map/aijk,bijk->ab/dot_general | solution.py:79
  104.5 44.6 %all-reduce.4 = (f32[16,16]{0,1:T(8,128)S(1)}, f32[16,16]{1,0:T(8,128)S(1)}) all-reduce(f32[16,16]{0,1:T(8,128)S(1)} %fusion.28, f32[16,16]{1,0:T(8,128)S(1)} %fusion.29), channel_id=1, replica_groups=mesh['gx'=4,'gy'=8] {'gx','gy'}, use_global_device_ids=true, to_apply=%region_1.2 | all-reduce | flops 512 | bytes 4096 | tf_op jit(solution)/shard_map/psum | solution.py:80
  149.1 1.5 cholesky.44
  150.6 0.6 compare_reduce_fusion.1
  151.3 0.6 fusion.44
  151.9 1.2 custom-call.10
  153.1 0.2 fusion.52
  153.9 1.5 cholesky.55
  155.4 0.6 compare_reduce_fusion
  156.1 0.6 fusion.45
  156.7 1.2 custom-call.11
  157.9 0.2 fusion.48
  158.3 0.2 fusion.68
  158.5 6.6 %fusion = f32[1,64,16,128]{3,0,2,1:T(1,128)S(1)} fusion(f32[8,64,16,128]{3,0,2,1:T(8,128)} %copy-done.5, f32[8,64,16,128]{3,0,2,1:T(8,128)} %copy-done.4, f32[16]{0:T(128)S(1)} %get-tuple-element.25), kind=kOutput, calls=%fused_computation.6 | convolution fusion | flops 27262976 | bytes 8912960 | tf_op jit(solution)/shard_map/a,aijk->ijk/dot_general | solution.py:85
  165.1 0.9 sub.83
  166.0 8.6 %copy_add_fusion = f32[8,64,16,128]{3,0,2,1:T(8,128)S(1)} fusion(f32[8,64,16,128]{3,2,1,0:T(8,128)} %param.13, f32[8,64,16,128]{3,0,2,1:T(8,128)S(1)} %copy-done.3, f32[8,64,16,128]{3,0,2,1:T(8,128)S(1)} %copy-done.1, f32[16,8]{0,1:T(8,128)S(1)} %get-tuple-element.26), kind=kOutput, calls=%fused_computation.50 | convolution fusion | flops 204472320 | bytes 16777728 | tf_op jit(solution)/shard_map/ab,aijk->bijk/dot_general | solution.py:83
  174.6 2.8 %copy.15 = f32[8,64,16,128]{3,2,1,0:T(8,128)} copy(f32[8,64,16,128]{3,0,2,1:T(8,128)S(1)} %copy_add_fusion) | data formatting | bytes 8388608
  (57 shorter events, 1.3 us)
Async XLA Ops:
  0.6 7.1 %copy-start.7 = (f32[64,16,128]{2,1,0:T(8,128)S(1)}, f32[64,16,128]{2,1,0:T(8,128)}, u32[]{:S(2)}) copy-start(f32[64,16,128]{2,1,0:T(8,128)} %param.11) | copy-start | bytes 1572868
  0.6 12.9 %copy-start.8 = (f32[64,16,128]{2,1,0:T(8,128)S(1)}, f32[64,16,128]{2,1,0:T(8,128)}, u32[]{:S(2)}) copy-start(f32[64,16,128]{2,1,0:T(8,128)} %param.10) | copy-start | bytes 1572868
  0.7 15.9 %copy-start.10 = (s32[64,16]{0,1:T(8,128)S(1)}, s32[64,16]{0,1:T(8,128)}, u32[]{:S(2)}) copy-start(s32[64,16]{0,1:T(8,128)} %param.14) | copy-start | bytes 12292
  0.7 28.0 %copy-start.6 = (f32[64,16,128]{2,1,0:T(8,128)S(1)}, f32[64,16,128]{2,1,0:T(8,128)}, u32[]{:S(2)}) copy-start(f32[64,16,128]{2,1,0:T(8,128)} %param.12) | copy-start | bytes 1572868
  0.7 28.0 %copy-start.9 = (f32[64,16,128]{2,1,0:T(8,128)S(1)}, f32[64,16,128]{2,1,0:T(8,128)}, u32[]{:S(2)}) copy-start(f32[64,16,128]{2,1,0:T(8,128)} %param.9) | copy-start | bytes 1572868
  3.4 13.3 %collective-permute-start = (f32[1,16,128]{2,1,0:T(8,128)S(1)}, f32[1,16,128]{2,1,0:T(8,128)S(1)}, u32[]{:S(2)}, u32[]{:S(2)}) collective-permute-start(f32[1,16,128]{2,1,0:T(8,128)S(1)} %get-tuple-element.24), channel_id=1, source_target_pairs={{8,0},{16,8},{24,16},{9,1},{17,9},{25,17},{10,2},{18,10},{26,18},{... | collective-permute-start | bytes 24584 | tf_op jit(solution)/shard_map/ppermute | solution.py:18
  4.7 12.0 %collective-permute-start.2 = (f32[1,16,128]{2,1,0:T(8,128)S(1)}, f32[1,16,128]{2,1,0:T(8,128)S(1)}, u32[]{:S(2)}, u32[]{:S(2)}) collective-permute-start(f32[1,16,128]{2,1,0:T(8,128)S(1)} %get-tuple-element.23), channel_id=1, source_target_pairs={{0,8},{8,16},{16,24},{1,9},{9,17},{17,25},{2,10},{10,18},{18,26},{... | collective-permute-start | bytes 24584 | tf_op jit(solution)/shard_map/ppermute | solution.py:15
  7.7 14.9 %collective-permute-start.4 = (f32[1,16,128]{2,1,0:T(8,128)S(1)}, f32[1,16,128]{2,1,0:T(8,128)S(1)}, u32[]{:S(2)}, u32[]{:S(2)}) collective-permute-start(f32[1,16,128]{2,1,0:T(8,128)S(1)} %get-tuple-element.22), channel_id=1, source_target_pairs={{0,8},{8,16},{16,24},{1,9},{9,17},{17,25},{2,10},{10,18},{18,26},{... | collective-permute-start | bytes 24584 | tf_op jit(solution)/shard_map/ppermute | solution.py:15
  12.2 10.4 %collective-permute-start.5 = (f32[1,16,128]{2,1,0:T(8,128)S(1)}, f32[1,16,128]{2,1,0:T(8,128)S(1)}, u32[]{:S(2)}, u32[]{:S(2)}) collective-permute-start(f32[1,16,128]{2,1,0:T(8,128)S(1)} %get-tuple-element.21), channel_id=1, source_target_pairs={{8,0},{16,8},{24,16},{9,1},{17,9},{25,17},{10,2},{18,10},{26,18},{... | collective-permute-start | bytes 24584 | tf_op jit(solution)/shard_map/ppermute | solution.py:18
  13.6 13.7 %collective-permute-start.1 = (f32[1,16,128]{2,1,0:T(8,128)S(1)}, f32[1,16,128]{2,1,0:T(8,128)S(1)}, u32[]{:S(2)}, u32[]{:S(2)}) collective-permute-start(f32[1,16,128]{2,1,0:T(8,128)S(1)} %slice.156), channel_id=1, source_target_pairs={{0,8},{8,16},{16,24},{1,9},{9,17},{17,25},{2,10},{10,18},{18,26},{... | collective-permute-start | bytes 24584 | tf_op jit(solution)/shard_map/ppermute | solution.py:15
  16.8 10.5 %collective-permute-start.3 = (f32[66,1,128]{2,1,0:T(1,128)S(1)}, f32[66,1,128]{2,1,0:T(1,128)S(1)}, u32[]{:S(2)}, u32[]{:S(2)}) collective-permute-start(f32[66,1,128]{2,1,0:T(1,128)S(1)} %get-tuple-element.19), channel_id=1, source_target_pairs={{1,0},{2,1},{3,2},{4,3},{5,4},{6,5},{7,6},{9,8},{10,9},{11,10},{12... | collective-permute-start | bytes 101384 | tf_op jit(solution)/shard_map/ppermute | solution.py:18
  18.1 9.2 %collective-permute-start.7 = (f32[66,1,128]{2,1,0:T(1,128)S(1)}, f32[66,1,128]{2,1,0:T(1,128)S(1)}, u32[]{:S(2)}, u32[]{:S(2)}) collective-permute-start(f32[66,1,128]{2,1,0:T(1,128)S(1)} %get-tuple-element.20), channel_id=1, source_target_pairs={{0,1},{1,2},{2,3},{3,4},{4,5},{5,6},{6,7},{8,9},{9,10},{10,11},{11... | collective-permute-start | bytes 101384 | tf_op jit(solution)/shard_map/ppermute | solution.py:15
  22.7 5.9 %collective-permute-start.6 = (f32[66,1,128]{2,1,0:T(1,128)S(1)}, f32[66,1,128]{2,1,0:T(1,128)S(1)}, u32[]{:S(2)}, u32[]{:S(2)}) collective-permute-start(f32[66,1,128]{2,1,0:T(1,128)S(1)} %slice.194), channel_id=1, source_target_pairs={{0,1},{1,2},{2,3},{3,4},{4,5},{5,6},{6,7},{8,9},{9,10},{10,11},{11... | collective-permute-start | bytes 101384 | tf_op jit(solution)/shard_map/ppermute | solution.py:15
  31.5 60.6 %copy-start = (f32[8,64,16,128]{3,0,2,1:T(8,128)}, f32[8,64,16,128]{3,0,2,1:T(8,128)S(1)}, u32[]{:S(2)}) copy-start(f32[8,64,16,128]{3,0,2,1:T(8,128)S(1)} %broadcast_multiply_fusion) | copy-start | bytes 12582916
  31.5 4.3 %collective-permute-start.8 = (f32[8,1,16,128]{3,0,2,1:T(8,128)S(1)}, f32[8,1,16,128]{3,0,2,1:T(8,128)S(1)}, u32[]{:S(2)}, u32[]{:S(2)}) collective-permute-start(f32[8,1,16,128]{3,0,2,1:T(8,128)S(1)} %get-tuple-element.18), channel_id=1, source_target_pairs={{8,0},{16,8},{24,16},{9,1},{17,9},{25,17},{10,2},{18,10},{26,18},{... | collective-permute-start | bytes 196616 | tf_op jit(solution)/shard_map/ppermute | solution.py:18
  32.8 3.9 %collective-permute-start.9 = (f32[8,1,16,128]{3,0,2,1:T(8,128)S(1)}, f32[8,1,16,128]{3,0,2,1:T(8,128)S(1)}, u32[]{:S(2)}, u32[]{:S(2)}) collective-permute-start(f32[8,1,16,128]{3,0,2,1:T(8,128)S(1)} %get-tuple-element.17), channel_id=1, source_target_pairs={{0,8},{8,16},{16,24},{1,9},{9,17},{17,25},{2,10},{10,18},{18,26},{... | collective-permute-start | bytes 196616 | tf_op jit(solution)/shard_map/ppermute | solution.py:15
  36.8 10.6 %collective-permute-start.10 = (f32[8,66,1,128]{3,0,2,1:T(8,128)S(1)}, f32[8,66,1,128]{3,0,2,1:T(8,128)S(1)}, u32[]{:S(2)}, u32[]{:S(2)}) collective-permute-start(f32[8,66,1,128]{3,0,2,1:T(8,128)S(1)} %get-tuple-element.13), channel_id=1, source_target_pairs={{1,0},{2,1},{3,2},{4,3},{5,4},{6,5},{7,6},{9,8},{10,9},{11,10},{12... | collective-permute-start | bytes 811016 | tf_op jit(solution)/shard_map/ppermute | solution.py:18
  38.1 16.6 %collective-permute-start.11 = (f32[8,66,1,128]{3,0,2,1:T(8,128)S(1)}, f32[8,66,1,128]{3,0,2,1:T(8,128)S(1)}, u32[]{:S(2)}, u32[]{:S(2)}) collective-permute-start(f32[8,66,1,128]{3,0,2,1:T(8,128)S(1)} %get-tuple-element.14), channel_id=1, source_target_pairs={{0,1},{1,2},{2,3},{3,4},{4,5},{5,6},{6,7},{8,9},{9,10},{10,11},{11... | collective-permute-start | bytes 811016 | tf_op jit(solution)/shard_map/ppermute | solution.py:15
  62.1 30.0 %copy-start.2 = (f32[8,64,16,128]{3,0,2,1:T(8,128)}, f32[8,64,16,128]{3,0,2,1:T(8,128)S(1)}, u32[]{:S(2)}) copy-start(f32[8,64,16,128]{3,0,2,1:T(8,128)S(1)} %get-tuple-element.7) | copy-start | bytes 12582916
  62.1 30.0 %copy-start.4 = (f32[8,64,16,128]{3,0,2,1:T(8,128)}, f32[8,64,16,128]{3,0,2,1:T(8,128)S(1)}, u32[]{:S(2)}) copy-start(f32[8,64,16,128]{3,0,2,1:T(8,128)S(1)} %get-tuple-element.8) | copy-start | bytes 12582916
  62.1 4.3 %collective-permute-start.12 = (f32[8,1,16,128]{3,0,2,1:T(8,128)S(1)}, f32[8,1,16,128]{3,0,2,1:T(8,128)S(1)}, u32[]{:S(2)}, u32[]{:S(2)}) collective-permute-start(f32[8,1,16,128]{3,0,2,1:T(8,128)S(1)} %get-tuple-element.16), channel_id=1, source_target_pairs={{8,0},{16,8},{24,16},{9,1},{17,9},{25,17},{10,2},{18,10},{26,18},{... | collective-permute-start | bytes 196616 | tf_op jit(solution)/shard_map/ppermute | solution.py:18
  63.4 3.9 %collective-permute-start.13 = (f32[8,1,16,128]{3,0,2,1:T(8,128)S(1)}, f32[8,1,16,128]{3,0,2,1:T(8,128)S(1)}, u32[]{:S(2)}, u32[]{:S(2)}) collective-permute-start(f32[8,1,16,128]{3,0,2,1:T(8,128)S(1)} %get-tuple-element.15), channel_id=1, source_target_pairs={{0,8},{8,16},{16,24},{1,9},{9,17},{17,25},{2,10},{10,18},{18,26},{... | collective-permute-start | bytes 196616 | tf_op jit(solution)/shard_map/ppermute | solution.py:15
  67.4 17.5 %collective-permute-start.14 = (f32[8,66,1,128]{3,0,2,1:T(8,128)S(1)}, f32[8,66,1,128]{3,0,2,1:T(8,128)S(1)}, u32[]{:S(2)}, u32[]{:S(2)}) collective-permute-start(f32[8,66,1,128]{3,0,2,1:T(8,128)S(1)} %get-tuple-element.11), channel_id=1, source_target_pairs={{1,0},{2,1},{3,2},{4,3},{5,4},{6,5},{7,6},{9,8},{10,9},{11,10},{12... | collective-permute-start | bytes 811016 | tf_op jit(solution)/shard_map/ppermute | solution.py:18
  68.7 16.6 %collective-permute-start.15 = (f32[8,66,1,128]{3,0,2,1:T(8,128)S(1)}, f32[8,66,1,128]{3,0,2,1:T(8,128)S(1)}, u32[]{:S(2)}, u32[]{:S(2)}) collective-permute-start(f32[8,66,1,128]{3,0,2,1:T(8,128)S(1)} %get-tuple-element.12), channel_id=1, source_target_pairs={{0,1},{1,2},{2,3},{3,4},{4,5},{5,6},{6,7},{8,9},{9,10},{10,11},{11... | collective-permute-start | bytes 811016 | tf_op jit(solution)/shard_map/ppermute | solution.py:15
  92.1 2.0 %copy-start.5 = (f32[8,64,16,128]{3,0,2,1:T(8,128)}, f32[8,64,16,128]{3,0,2,1:T(8,128)S(1)}, u32[]{:S(2)}) copy-start(f32[8,64,16,128]{3,0,2,1:T(8,128)S(1)} %fusion.10) | copy-start | bytes 12582916
  158.5 7.5 %copy-start.1 = (f32[8,64,16,128]{3,0,2,1:T(8,128)S(1)}, f32[8,64,16,128]{3,0,2,1:T(8,128)}, u32[]{:S(2)}) copy-start(f32[8,64,16,128]{3,0,2,1:T(8,128)} %copy-done) | copy-start | bytes 12582916
  158.5 7.5 %copy-start.3 = (f32[8,64,16,128]{3,0,2,1:T(8,128)S(1)}, f32[8,64,16,128]{3,0,2,1:T(8,128)}, u32[]{:S(2)}) copy-start(f32[8,64,16,128]{3,0,2,1:T(8,128)} %copy-done.2) | copy-start | bytes 12582916
where the time goes:
time: 178 us; the launch traced here: 177 us
  starting transfers between devices  44.6 us (25%)
  blocking collectives  44.6 us (25%)
  matrix products  37.9 us (21%)
  other arithmetic  29 us (16%)
  waiting for transfers between devices  14.8 us (8%)
  local copies, waits for them, and re-layouts  5.36 us (3%)
    psum x1, blocking collectives, shards(): gram = lax.psum(gram_local, ('gx', 'gy'))  44.6 us
    ppermute x9, starting transfers between devices, padded_2(): lax.ppermute(lax.slice_in_dim(block, block.shape[dim] - width, None, axis...  35.5 us
    dot_general x1, matrix products, shards(): gram_local = jnp.einsum('aijk,bijk->ab', basis, basis, precision=highest)  11.2 us
    ppermute x9, waiting for transfers between devices, padded_2(): lax.ppermute(lax.slice_in_dim(block, block.shape[dim] - width, None, axis...  10.7 us
    dot_general x1, matrix products, shards(): project_local = jnp.einsum('aijk,bijk->ab', basis, image, precision=highest)  10.4 us
    ppermute x7, starting transfers between devices, padded_2(): lax.ppermute(lax.slice_in_dim(block, 0, width, axis=dim), axis, backward)  9.04 us
    dot_general x1, matrix products, shards(): jnp.einsum('ab,aijk->bijk', coeffs, basis, precision=highest)  8.56 us
    sub x1, other arithmetic, shards(): powered = applied - basis_shift * blocks  7.45 us
  transfers between devices with their start and end apart: 16, of which 6 were waited for; matrix products, arithmetic and copies ran while one was open for 7% of the time, Pallas kernels for 0%

commit v1 on v0

--- a/solution.py
+++ b/solution.py
@@ -2,6 +2,7 @@
 import jax.numpy as jnp
 from jax import lax
 from jax.sharding import PartitionSpec as P
+from jax.lax import psum
 
 ENLARGE = 8
 basis_shift = 6.5
@@ -77,7 +78,7 @@
     image = jnp.concatenate([applied, second], axis=0)
     gram_local = jnp.einsum("aijk,bijk->ab", basis, basis, precision=highest)
     project_local = jnp.einsum("aijk,bijk->ab", basis, image, precision=highest)
-    gram = lax.psum(gram_local, ("gx", "gy"))
+    gram = psum(psum(gram_local, "gx"), axis_name="gy")
     project = lax.psum(project_local, ("gx", "gy"))
     coeffs = finish(gram, project)
     new_iterates = iterates + jnp.einsum("ab,aijk->bijk", coeffs, basis, precision=highest)

time: 178 us -> 207 us (1.16)
  blocking collectives: 44.6 us -> 67.5 us
  other arithmetic: 29 us -> 32.1 us
  waiting for transfers between devices: 14.8 us -> 17.7 us
    psum x1 -> x3, blocking collectives: 44.6 us -> 67.5 us  [the longest x1 40.2 us: shards(): project = lax.psum(project_local, ('gx', 'gy'))]
    unnamed x26 -> x36, local copies, waits for them, and re-layouts: 4.88 us -> 4.92 us
  transfers between devices with their start and end apart: 16 -> 16, of which waited for: 6 -> 6; matrix products, arithmetic and copies ran while one was open for 7% -> 2% of each run, Pallas kernels for 0% -> 0%
where the time goes in v1:
time: 207 us; the launch traced here: 206 us
  blocking collectives  67.5 us (33%)
  starting transfers between devices  44.6 us (22%)
  matrix products  37.8 us (18%)
  other arithmetic  32.1 us (16%)
  waiting for transfers between devices  17.7 us (9%)
  local copies, waits for them, and re-layouts  5.41 us (3%)
    psum x1, blocking collectives, shards(): project = lax.psum(project_local, ('gx', 'gy'))  40.2 us
    ppermute x9, starting transfers between devices, padded_2(): lax.ppermute(lax.slice_in_dim(block, block.shape[dim] - width, None, axis...  35.1 us
    psum x2, blocking collectives, shards(): gram = psum(psum(gram_local, 'gx'), axis_name='gy')  27.3 us
    ppermute x9, waiting for transfers between devices, padded_2(): lax.ppermute(lax.slice_in_dim(block, block.shape[dim] - width, None, axis...  11.7 us
    dot_general x1, matrix products, shards(): gram_local = jnp.einsum('aijk,bijk->ab', basis, basis, precision=highest)  11.2 us
    dot_general x1, matrix products, shards(): project_local = jnp.einsum('aijk,bijk->ab', basis, image, precision=highest)  10.4 us
    ppermute x7, starting transfers between devices, padded_2(): lax.ppermute(lax.slice_in_dim(block, 0, width, axis=dim), axis, backward)  9.5 us
    dot_general x1, matrix products, shards(): jnp.einsum('ab,aijk->bijk', coeffs, basis, precision=highest)  8.56 us
  transfers between devices with their start and end apart: 16, of which 6 were waited for; matrix products, arithmetic and copies ran while one was open for 2% of the time, Pallas kernels for 0%

profile of v1, /device:TPU:0, one launch (start us, length us, event | category | flops | bytes accessed | tf_op | source)
XLA Modules:
  0.0 206.2 jit_solution(17266462612329100155)
XLA Ops:
  0.7 2.7 %reduce_sum.18 = f32[64,16,128]{2,1,0:T(8,128)S(1)} reduce(f32[8,64,16,128]{3,2,1,0:T(8,128)} %param.13, f32[]{:T(128)} %constant.43.clone.1), dimensions={0}, to_apply=%region_0.0 | reduce | flops 917504 | bytes 4718596 | tf_op jit(solution)/shard_map/reduce_sum | solution.py:61
  3.4 1.3 collective-permute-start
  4.7 3.0 %collective-permute-start.2 = (f32[1,16,128]{2,1,0:T(8,128)S(1)}, f32[1,16,128]{2,1,0:T(8,128)S(1)}, u32[]{:S(2)}, u32[]{:S(2)}) collective-permute-start(f32[1,16,128]{2,1,0:T(8,128)S(1)} %get-tuple-element.21), channel_id=1, source_target_pairs={{0,8},{8,16},{16,24},{1,9},{9,17},{17,25},{2,10},{10,18},{18,26},{... | collective-permute-start | bytes 24584 | tf_op jit(solution)/shard_map/ppermute | solution.py:16
  7.7 4.5 %collective-permute-start.4 = (f32[1,16,128]{2,1,0:T(8,128)S(1)}, f32[1,16,128]{2,1,0:T(8,128)S(1)}, u32[]{:S(2)}, u32[]{:S(2)}) collective-permute-start(f32[1,16,128]{2,1,0:T(8,128)S(1)} %get-tuple-element.20), channel_id=1, source_target_pairs={{0,8},{8,16},{16,24},{1,9},{9,17},{17,25},{2,10},{10,18},{18,26},{... | collective-permute-start | bytes 24584 | tf_op jit(solution)/shard_map/ppermute | solution.py:16
  12.2 1.3 collective-permute-start.5
  13.6 3.0 %collective-permute-start.1 = (f32[1,16,128]{2,1,0:T(8,128)S(1)}, f32[1,16,128]{2,1,0:T(8,128)S(1)}, u32[]{:S(2)}, u32[]{:S(2)}) collective-permute-start(f32[1,16,128]{2,1,0:T(8,128)S(1)} %slice.156), channel_id=1, source_target_pairs={{0,8},{8,16},{16,24},{1,9},{9,17},{17,25},{2,10},{10,18},{18,26},{... | collective-permute-start | bytes 24584 | tf_op jit(solution)/shard_map/ppermute | solution.py:16
  16.8 1.3 collective-permute-start.3
  18.1 4.5 %collective-permute-start.7 = (f32[66,1,128]{2,1,0:T(1,128)S(1)}, f32[66,1,128]{2,1,0:T(1,128)S(1)}, u32[]{:S(2)}, u32[]{:S(2)}) collective-permute-start(f32[66,1,128]{2,1,0:T(1,128)S(1)} %get-tuple-element.18), channel_id=1, source_target_pairs={{0,1},{1,2},{2,3},{3,4},{4,5},{5,6},{6,7},{8,9},{9,10},{10,11},{11... | collective-permute-start | bytes 101384 | tf_op jit(solution)/shard_map/ppermute | solution.py:16
  22.7 4.3 %collective-permute-start.6 = (f32[66,1,128]{2,1,0:T(1,128)S(1)}, f32[66,1,128]{2,1,0:T(1,128)S(1)}, u32[]{:S(2)}, u32[]{:S(2)}) collective-permute-start(f32[66,1,128]{2,1,0:T(1,128)S(1)} %slice.194), channel_id=1, source_target_pairs={{0,1},{1,2},{2,3},{3,4},{4,5},{5,6},{6,7},{8,9},{9,10},{10,11},{11... | collective-permute-start | bytes 101384 | tf_op jit(solution)/shard_map/ppermute | solution.py:16
  27.3 1.3 collective-permute-done.6
  28.6 1.6 fusion.33
  30.2 1.3 broadcast_multiply_fusion
  31.5 1.4 collective-permute-start.8
  33.0 3.0 %collective-permute-start.9 = (f32[8,1,16,128]{3,0,2,1:T(8,128)S(1)}, f32[8,1,16,128]{3,0,2,1:T(8,128)S(1)}, u32[]{:S(2)}, u32[]{:S(2)}) collective-permute-start(f32[8,1,16,128]{3,0,2,1:T(8,128)S(1)} %get-tuple-element.15), channel_id=1, source_target_pairs={{0,8},{8,16},{16,24},{1,9},{9,17},{17,25},{2,10},{10,18},{18,26},{... | collective-permute-start | bytes 196616 | tf_op jit(solution)/shard_map/ppermute | solution.py:16
  36.0 0.9 collective-permute-done.9
  36.9 1.3 collective-permute-start.10
  38.2 5.0 %collective-permute-start.11 = (f32[8,66,1,128]{3,0,2,1:T(8,128)S(1)}, f32[8,66,1,128]{3,0,2,1:T(8,128)S(1)}, u32[]{:S(2)}, u32[]{:S(2)}) collective-permute-start(f32[8,66,1,128]{3,0,2,1:T(8,128)S(1)} %get-tuple-element.12), channel_id=1, source_target_pairs={{0,1},{1,2},{2,3},{3,4},{4,5},{5,6},{6,7},{8,9},{9,10},{10,11},{11... | collective-permute-start | bytes 811016 | tf_op jit(solution)/shard_map/ppermute | solution.py:16
  43.5 4.0 %collective-permute-done.10 = f32[8,66,1,128]{3,0,2,1:T(8,128)S(1)} collective-permute-done((f32[8,66,1,128]{3,0,2,1:T(8,128)S(1)}, f32[8,66,1,128]{3,0,2,1:T(8,128)S(1)}, u32[]{:S(2)}, u32[]{:S(2)}) %collective-permute-start.10) | collective-permute-done | bytes 270368 | tf_op jit(solution)/shard_map/ppermute | solution.py:19
  47.6 7.2 %collective-permute-done.11 = f32[8,66,1,128]{3,0,2,1:T(8,128)S(1)} collective-permute-done((f32[8,66,1,128]{3,0,2,1:T(8,128)S(1)}, f32[8,66,1,128]{3,0,2,1:T(8,128)S(1)}, u32[]{:S(2)}, u32[]{:S(2)}) %collective-permute-start.11) | collective-permute-done | bytes 270368 | tf_op jit(solution)/shard_map/ppermute | solution.py:16
  54.8 8.3 %multiply_subtract_fusion = (f32[8,64,16,128]{3,0,2,1:T(8,128)S(1)}, f32[8,64,16,128]{3,0,2,1:T(8,128)}) fusion(f32[8,64,16]{0,2,1:T(8,128)S(1)} %fusion.43, f32[64,16,128]{2,1,0:T(8,128)S(1)} %get-tuple-element.7, f32[64,16,128]{2,1,0:T(8,128)S(1)} %pad.18, f32[8,64,16,128]{3,0,2,1:T(8,128)S(1)} %broadcast_multiply_fusion, f32[64,16,128]{2,1,0:T(8,128)S(1)} %copy-done.8, ...), kind=kLoop, calls=%fused_computation.51 | loop fusion | flops 25165824 | bytes 17481728 | tf_op jit(solution)/shard_map/sub | solution.py:74
  63.1 11.2 %fusion.28 = f32[16,16]{0,1:T(8,128)S(1)} fusion(f32[8,64,16,128]{3,0,2,1:T(8,128)S(1)} %get-tuple-element.5, f32[8,64,16,128]{3,0,2,1:T(8,128)S(1)} %broadcast_multiply_fusion), kind=kOutput, calls=%fused_computation.55 | convolution fusion | flops 404750336 | bytes 8389632 | tf_op jit(solution)/shard_map/aijk,bijk->ab/dot_general | solution.py:79
  74.3 1.3 collective-permute-start.12
  75.6 3.0 %collective-permute-start.13 = (f32[8,1,16,128]{3,0,2,1:T(8,128)S(1)}, f32[8,1,16,128]{3,0,2,1:T(8,128)S(1)}, u32[]{:S(2)}, u32[]{:S(2)}) collective-permute-start(f32[8,1,16,128]{3,0,2,1:T(8,128)S(1)} %get-tuple-element.13), channel_id=1, source_target_pairs={{0,8},{8,16},{16,24},{1,9},{9,17},{17,25},{2,10},{10,18},{18,26},{... | collective-permute-start | bytes 196616 | tf_op jit(solution)/shard_map/ppermute | solution.py:16
  78.6 7.3 %psum.21 = f32[16,16]{0,1:T(8,128)S(1)} all-reduce(f32[16,16]{0,1:T(8,128)S(1)} %fusion.28), channel_id=1, replica_groups=mesh['gx'=4,'gy'=8] {'gx'}, use_global_device_ids=true, to_apply=%region_1.2 | all-reduce | flops 256 | bytes 2048 | tf_op jit(solution)/shard_map/psum | solution.py:81
  85.9 20.0 %psum.22 = f32[16,16]{0,1:T(8,128)S(1)} all-reduce(f32[16,16]{0,1:T(8,128)S(1)} %psum.21), channel_id=1, replica_groups=mesh['gx'=4,'gy'=8] {'gy'}, use_global_device_ids=true, to_apply=%region_2.3 | all-reduce | flops 256 | bytes 2048 | tf_op jit(solution)/shard_map/psum | solution.py:81
  106.0 1.5 cholesky.44
  107.5 0.7 compare_reduce_fusion.1
  108.2 0.6 fusion.44
  108.8 1.2 custom-call.10
  110.1 1.2 pad_maximum_fusion.43
  111.3 1.6 collective-permute-start.14
  112.9 4.6 %collective-permute-start.15 = (f32[8,66,1,128]{3,0,2,1:T(8,128)S(1)}, f32[8,66,1,128]{3,0,2,1:T(8,128)S(1)}, u32[]{:S(2)}, u32[]{:S(2)}) collective-permute-start(f32[8,66,1,128]{3,0,2,1:T(8,128)S(1)} %get-tuple-element.10), channel_id=1, source_target_pairs={{0,1},{1,2},{2,3},{3,4},{4,5},{5,6},{6,7},{8,9},{9,10},{10,11},{11... | collective-permute-start | bytes 811016 | tf_op jit(solution)/shard_map/ppermute | solution.py:16
  117.8 2.0 collective-permute-done.14
  119.8 2.2 %collective-permute-done.15 = f32[8,66,1,128]{3,0,2,1:T(8,128)S(1)} collective-permute-done((f32[8,66,1,128]{3,0,2,1:T(8,128)S(1)}, f32[8,66,1,128]{3,0,2,1:T(8,128)S(1)}, u32[]{:S(2)}, u32[]{:S(2)}) %collective-permute-start.15) | collective-permute-done | bytes 270368 | tf_op jit(solution)/shard_map/ppermute | solution.py:16
  122.0 7.9 %fusion.10 = f32[8,64,16,128]{3,0,2,1:T(8,128)S(1)} fusion(f32[8,64,16,128]{3,0,2,1:T(8,128)S(1)} %copy-done.4, f32[8,66,1,128]{3,0,2,1:T(8,128)S(1)} %collective-permute-done.15, f32[8,1,16,128]{3,0,2,1:T(8,128)S(1)} %collective-permute-done.12, f32[8,1,16,128]{3,0,2,1:T(8,128)S(1)} %collective-permute-done.13, ...), kind=kLoop, calls=%fused_computation.16 | loop fusion | flops 22020096 | bytes 12730368 | tf_op jit(solution)/shard_map/sub | solution.py:40
  129.9 2.0 copy-done.7
  131.8 10.4 %fusion.29 = f32[16,16]{1,0:T(8,128)S(1)} fusion(f32[8,64,16,128]{3,0,2,1:T(8,128)S(1)} %fusion.10, f32[8,64,16,128]{3,0,2,1:T(8,128)S(1)} %copy-done.6, f32[8,64,16,128]{3,0,2,1:T(8,128)S(1)} %copy-done.4, f32[8,64,16,128]{3,0,2,1:T(8,128)S(1)} %copy-done.1), kind=kOutput, calls=%fused_computation.56 | convolution fusion | flops 406847488 | bytes 16778240 | tf_op jit(solution)/shard_map/aijk,bijk->ab/dot_general | solution.py:80
  142.2 40.2 %psum.23 = f32[16,16]{1,0:T(8,128)S(1)} all-reduce(f32[16,16]{1,0:T(8,128)S(1)} %fusion.29), channel_id=1, replica_groups=mesh['gx'=4,'gy'=8] {'gx','gy'}, use_global_device_ids=true, to_apply=%region_5.7 | all-reduce | flops 256 | bytes 2048 | tf_op jit(solution)/shard_map/psum | solution.py:82
  182.8 1.5 cholesky.55
  184.3 0.6 compare_reduce_fusion
  184.9 0.6 fusion.45
  185.6 1.2 custom-call.11
  186.8 0.2 fusion.48
  187.2 0.2 fusion.68
  187.4 6.6 %fusion = f32[1,64,16,128]{3,0,2,1:T(1,128)S(1)} fusion(f32[8,64,16,128]{3,0,2,1:T(8,128)} %copy-done.7, f32[8,64,16,128]{3,0,2,1:T(8,128)} %get-tuple-element.6, f32[16]{0:T(128)S(1)} %get-tuple-element.23), kind=kOutput, calls=%fused_computation.6 | convolution fusion | flops 27262976 | bytes 8912960 | tf_op jit(solution)/shard_map/a,aijk->ijk/dot_general | solution.py:86
  194.0 0.9 sub.83
  194.9 8.6 %copy_add_fusion = f32[8,64,16,128]{3,0,2,1:T(8,128)S(1)} fusion(f32[8,64,16,128]{3,2,1,0:T(8,128)} %param.13, f32[8,64,16,128]{3,0,2,1:T(8,128)S(1)} %copy-done.5, f32[8,64,16,128]{3,0,2,1:T(8,128)S(1)} %copy-done.2, f32[16,8]{0,1:T(8,128)S(1)} %get-tuple-element.24), kind=kOutput, calls=%fused_computation.50 | convolution fusion | flops 204472320 | bytes 16777728 | tf_op jit(solution)/shard_map/ab,aijk->bijk/dot_general | solution.py:84
  203.4 2.8 %copy.15 = f32[8,64,16,128]{3,2,1,0:T(8,128)} copy(f32[8,64,16,128]{3,0,2,1:T(8,128)S(1)} %copy_add_fusion) | data formatting | bytes 8388608
  (69 shorter events, 1.8 us)
Async XLA Ops:
  0.6 7.1 %copy-start.9 = (f32[64,16,128]{2,1,0:T(8,128)S(1)}, f32[64,16,128]{2,1,0:T(8,128)}, u32[]{:S(2)}) copy-start(f32[64,16,128]{2,1,0:T(8,128)} %param.11) | copy-start | bytes 1572868
  0.6 12.9 %copy-start.10 = (f32[64,16,128]{2,1,0:T(8,128)S(1)}, f32[64,16,128]{2,1,0:T(8,128)}, u32[]{:S(2)}) copy-start(f32[64,16,128]{2,1,0:T(8,128)} %param.10) | copy-start | bytes 1572868
  0.7 16.0 %copy-start.15 = (s32[64,16]{0,1:T(8,128)S(1)}, s32[64,16]{0,1:T(8,128)}, u32[]{:S(2)}) copy-start(s32[64,16]{0,1:T(8,128)} %param.14) | copy-start | bytes 12292
  0.7 28.0 %copy-start.8 = (f32[64,16,128]{2,1,0:T(8,128)S(1)}, f32[64,16,128]{2,1,0:T(8,128)}, u32[]{:S(2)}) copy-start(f32[64,16,128]{2,1,0:T(8,128)} %param.12) | copy-start | bytes 1572868
  0.7 28.0 %copy-start.11 = (f32[64,16,128]{2,1,0:T(8,128)S(1)}, f32[64,16,128]{2,1,0:T(8,128)}, u32[]{:S(2)}) copy-start(f32[64,16,128]{2,1,0:T(8,128)} %param.9) | copy-start | bytes 1572868
  3.4 13.3 %collective-permute-start = (f32[1,16,128]{2,1,0:T(8,128)S(1)}, f32[1,16,128]{2,1,0:T(8,128)S(1)}, u32[]{:S(2)}, u32[]{:S(2)}) collective-permute-start(f32[1,16,128]{2,1,0:T(8,128)S(1)} %get-tuple-element.22), channel_id=1, source_target_pairs={{8,0},{16,8},{24,16},{9,1},{17,9},{25,17},{10,2},{18,10},{26,18},{... | collective-permute-start | bytes 24584 | tf_op jit(solution)/shard_map/ppermute | solution.py:19
  4.7 12.0 %collective-permute-start.2 = (f32[1,16,128]{2,1,0:T(8,128)S(1)}, f32[1,16,128]{2,1,0:T(8,128)S(1)}, u32[]{:S(2)}, u32[]{:S(2)}) collective-permute-start(f32[1,16,128]{2,1,0:T(8,128)S(1)} %get-tuple-element.21), channel_id=1, source_target_pairs={{0,8},{8,16},{16,24},{1,9},{9,17},{17,25},{2,10},{10,18},{18,26},{... | collective-permute-start | bytes 24584 | tf_op jit(solution)/shard_map/ppermute | solution.py:16
  7.7 14.9 %collective-permute-start.4 = (f32[1,16,128]{2,1,0:T(8,128)S(1)}, f32[1,16,128]{2,1,0:T(8,128)S(1)}, u32[]{:S(2)}, u32[]{:S(2)}) collective-permute-start(f32[1,16,128]{2,1,0:T(8,128)S(1)} %get-tuple-element.20), channel_id=1, source_target_pairs={{0,8},{8,16},{16,24},{1,9},{9,17},{17,25},{2,10},{10,18},{18,26},{... | collective-permute-start | bytes 24584 | tf_op jit(solution)/shard_map/ppermute | solution.py:16
  12.2 10.4 %collective-permute-start.5 = (f32[1,16,128]{2,1,0:T(8,128)S(1)}, f32[1,16,128]{2,1,0:T(8,128)S(1)}, u32[]{:S(2)}, u32[]{:S(2)}) collective-permute-start(f32[1,16,128]{2,1,0:T(8,128)S(1)} %get-tuple-element.19), channel_id=1, source_target_pairs={{8,0},{16,8},{24,16},{9,1},{17,9},{25,17},{10,2},{18,10},{26,18},{... | collective-permute-start | bytes 24584 | tf_op jit(solution)/shard_map/ppermute | solution.py:19
  13.6 13.7 %collective-permute-start.1 = (f32[1,16,128]{2,1,0:T(8,128)S(1)}, f32[1,16,128]{2,1,0:T(8,128)S(1)}, u32[]{:S(2)}, u32[]{:S(2)}) collective-permute-start(f32[1,16,128]{2,1,0:T(8,128)S(1)} %slice.156), channel_id=1, source_target_pairs={{0,8},{8,16},{16,24},{1,9},{9,17},{17,25},{2,10},{10,18},{18,26},{... | collective-permute-start | bytes 24584 | tf_op jit(solution)/shard_map/ppermute | solution.py:16
  16.8 10.5 %collective-permute-start.3 = (f32[66,1,128]{2,1,0:T(1,128)S(1)}, f32[66,1,128]{2,1,0:T(1,128)S(1)}, u32[]{:S(2)}, u32[]{:S(2)}) collective-permute-start(f32[66,1,128]{2,1,0:T(1,128)S(1)} %get-tuple-element.17), channel_id=1, source_target_pairs={{1,0},{2,1},{3,2},{4,3},{5,4},{6,5},{7,6},{9,8},{10,9},{11,10},{12... | collective-permute-start | bytes 101384 | tf_op jit(solution)/shard_map/ppermute | solution.py:19
  18.1 9.2 %collective-permute-start.7 = (f32[66,1,128]{2,1,0:T(1,128)S(1)}, f32[66,1,128]{2,1,0:T(1,128)S(1)}, u32[]{:S(2)}, u32[]{:S(2)}) collective-permute-start(f32[66,1,128]{2,1,0:T(1,128)S(1)} %get-tuple-element.18), channel_id=1, source_target_pairs={{0,1},{1,2},{2,3},{3,4},{4,5},{5,6},{6,7},{8,9},{9,10},{10,11},{11... | collective-permute-start | bytes 101384 | tf_op jit(solution)/shard_map/ppermute | solution.py:16
  22.7 5.9 %collective-permute-start.6 = (f32[66,1,128]{2,1,0:T(1,128)S(1)}, f32[66,1,128]{2,1,0:T(1,128)S(1)}, u32[]{:S(2)}, u32[]{:S(2)}) collective-permute-start(f32[66,1,128]{2,1,0:T(1,128)S(1)} %slice.194), channel_id=1, source_target_pairs={{0,1},{1,2},{2,3},{3,4},{4,5},{5,6},{6,7},{8,9},{9,10},{10,11},{11... | collective-permute-start | bytes 101384 | tf_op jit(solution)/shard_map/ppermute | solution.py:16
  30.2 24.6 %copy-start.14 = (f32[64,16,128]{2,1,0:T(8,128)}, f32[64,16,128]{2,1,0:T(8,128)S(1)}, u32[]{:S(2)}) copy-start(f32[64,16,128]{2,1,0:T(8,128)S(1)} %get-tuple-element.8) | copy-start | bytes 1572868
  31.5 31.6 %copy-start = (f32[8,64,16,128]{3,0,2,1:T(8,128)}, f32[8,64,16,128]{3,0,2,1:T(8,128)S(1)}, u32[]{:S(2)}) copy-start(f32[8,64,16,128]{3,0,2,1:T(8,128)S(1)} %broadcast_multiply_fusion) | copy-start | bytes 12582916
  31.5 23.3 %copy-start.12 = (f32[64,16,128]{2,1,0:T(8,128)S(1)}, f32[64,16,128]{2,1,0:T(8,128)}, u32[]{:S(2)}) copy-start(f32[64,16,128]{2,1,0:T(8,128)} %param.9) | copy-start | bytes 1572868
  31.5 4.5 %collective-permute-start.8 = (f32[8,1,16,128]{3,0,2,1:T(8,128)S(1)}, f32[8,1,16,128]{3,0,2,1:T(8,128)S(1)}, u32[]{:S(2)}, u32[]{:S(2)}) collective-permute-start(f32[8,1,16,128]{3,0,2,1:T(8,128)S(1)} %get-tuple-element.16), channel_id=1, source_target_pairs={{8,0},{16,8},{24,16},{9,1},{17,9},{25,17},{10,2},{18,10},{26,18},{... | collective-permute-start | bytes 196616 | tf_op jit(solution)/shard_map/ppermute | solution.py:19
  33.0 3.9 %collective-permute-start.9 = (f32[8,1,16,128]{3,0,2,1:T(8,128)S(1)}, f32[8,1,16,128]{3,0,2,1:T(8,128)S(1)}, u32[]{:S(2)}, u32[]{:S(2)}) collective-permute-start(f32[8,1,16,128]{3,0,2,1:T(8,128)S(1)} %get-tuple-element.15), channel_id=1, source_target_pairs={{0,8},{8,16},{16,24},{1,9},{9,17},{17,25},{2,10},{10,18},{18,26},{... | collective-permute-start | bytes 196616 | tf_op jit(solution)/shard_map/ppermute | solution.py:16
  36.9 10.6 %collective-permute-start.10 = (f32[8,66,1,128]{3,0,2,1:T(8,128)S(1)}, f32[8,66,1,128]{3,0,2,1:T(8,128)S(1)}, u32[]{:S(2)}, u32[]{:S(2)}) collective-permute-start(f32[8,66,1,128]{3,0,2,1:T(8,128)S(1)} %get-tuple-element.11), channel_id=1, source_target_pairs={{1,0},{2,1},{3,2},{4,3},{5,4},{6,5},{7,6},{9,8},{10,9},{11,10},{12... | collective-permute-start | bytes 811016 | tf_op jit(solution)/shard_map/ppermute | solution.py:19
  38.2 16.6 %collective-permute-start.11 = (f32[8,66,1,128]{3,0,2,1:T(8,128)S(1)}, f32[8,66,1,128]{3,0,2,1:T(8,128)S(1)}, u32[]{:S(2)}, u32[]{:S(2)}) collective-permute-start(f32[8,66,1,128]{3,0,2,1:T(8,128)S(1)} %get-tuple-element.12), channel_id=1, source_target_pairs={{0,1},{1,2},{2,3},{3,4},{4,5},{5,6},{6,7},{8,9},{9,10},{10,11},{11... | collective-permute-start | bytes 811016 | tf_op jit(solution)/shard_map/ppermute | solution.py:16
  63.1 11.2 %copy-start.3 = (f32[8,64,16,128]{3,0,2,1:T(8,128)}, f32[8,64,16,128]{3,0,2,1:T(8,128)S(1)}, u32[]{:S(2)}) copy-start(f32[8,64,16,128]{3,0,2,1:T(8,128)S(1)} %get-tuple-element.5) | copy-start | bytes 12582916
  74.3 35.8 %collective-permute-start.12 = (f32[8,1,16,128]{3,0,2,1:T(8,128)S(1)}, f32[8,1,16,128]{3,0,2,1:T(8,128)S(1)}, u32[]{:S(2)}, u32[]{:S(2)}) collective-permute-start(f32[8,1,16,128]{3,0,2,1:T(8,128)S(1)} %get-tuple-element.14), channel_id=1, source_target_pairs={{8,0},{16,8},{24,16},{9,1},{17,9},{25,17},{10,2},{18,10},{26,18},{... | collective-permute-start | bytes 196616 | tf_op jit(solution)/shard_map/ppermute | solution.py:19
  75.6 34.5 %collective-permute-start.13 = (f32[8,1,16,128]{3,0,2,1:T(8,128)S(1)}, f32[8,1,16,128]{3,0,2,1:T(8,128)S(1)}, u32[]{:S(2)}, u32[]{:S(2)}) collective-permute-start(f32[8,1,16,128]{3,0,2,1:T(8,128)S(1)} %get-tuple-element.13), channel_id=1, source_target_pairs={{0,8},{8,16},{16,24},{1,9},{9,17},{17,25},{2,10},{10,18},{18,26},{... | collective-permute-start | bytes 196616 | tf_op jit(solution)/shard_map/ppermute | solution.py:16
  110.0 11.9 %copy-start.4 = (f32[8,64,16,128]{3,0,2,1:T(8,128)S(1)}, f32[8,64,16,128]{3,0,2,1:T(8,128)}, u32[]{:S(2)}) copy-start(f32[8,64,16,128]{3,0,2,1:T(8,128)} %copy-done.3) | copy-start | bytes 12582916
  110.1 11.9 %copy-start.13 = (f32[64,16,128]{2,1,0:T(8,128)S(1)}, f32[64,16,128]{2,1,0:T(8,128)}, u32[]{:S(2)}) copy-start(f32[64,16,128]{2,1,0:T(8,128)} %param.9) | copy-start | bytes 1572868
  111.3 8.5 %collective-permute-start.14 = (f32[8,66,1,128]{3,0,2,1:T(8,128)S(1)}, f32[8,66,1,128]{3,0,2,1:T(8,128)S(1)}, u32[]{:S(2)}, u32[]{:S(2)}) collective-permute-start(f32[8,66,1,128]{3,0,2,1:T(8,128)S(1)} %get-tuple-element.9), channel_id=1, source_target_pairs={{1,0},{2,1},{3,2},{4,3},{5,4},{6,5},{7,6},{9,8},{10,9},{11,10},{12... | collective-permute-start | bytes 811016 | tf_op jit(solution)/shard_map/ppermute | solution.py:19
  112.9 9.1 %collective-permute-start.15 = (f32[8,66,1,128]{3,0,2,1:T(8,128)S(1)}, f32[8,66,1,128]{3,0,2,1:T(8,128)S(1)}, u32[]{:S(2)}, u32[]{:S(2)}) collective-permute-start(f32[8,66,1,128]{3,0,2,1:T(8,128)S(1)} %get-tuple-element.10), channel_id=1, source_target_pairs={{0,1},{1,2},{2,3},{3,4},{4,5},{5,6},{6,7},{8,9},{9,10},{10,11},{11... | collective-permute-start | bytes 811016 | tf_op jit(solution)/shard_map/ppermute | solution.py:16
  117.8 14.0 %copy-start.1 = (f32[8,64,16,128]{3,0,2,1:T(8,128)S(1)}, f32[8,64,16,128]{3,0,2,1:T(8,128)}, u32[]{:S(2)}) copy-start(f32[8,64,16,128]{3,0,2,1:T(8,128)} %copy-done) | copy-start | bytes 12582916
  117.8 14.0 %copy-start.6 = (f32[8,64,16,128]{3,0,2,1:T(8,128)S(1)}, f32[8,64,16,128]{3,0,2,1:T(8,128)}, u32[]{:S(2)}) copy-start(f32[8,64,16,128]{3,0,2,1:T(8,128)} %get-tuple-element.6) | copy-start | bytes 12582916
  129.9 2.0 copy-start.7
  187.4 7.5 %copy-start.2 = (f32[8,64,16,128]{3,0,2,1:T(8,128)S(1)}, f32[8,64,16,128]{3,0,2,1:T(8,128)}, u32[]{:S(2)}) copy-start(f32[8,64,16,128]{3,0,2,1:T(8,128)} %copy-done) | copy-start | bytes 12582916
  187.4 7.5 %copy-start.5 = (f32[8,64,16,128]{3,0,2,1:T(8,128)S(1)}, f32[8,64,16,128]{3,0,2,1:T(8,128)}, u32[]{:S(2)}) copy-start(f32[8,64,16,128]{3,0,2,1:T(8,128)} %copy-done.3) | copy-start | bytes 12582916
